TPU v7x, 32 devices: a whole 2x2x4 slice. The times are simulated.
32 devices in a mesh: region: 4 (over y, x), cluster: 8 (over z, core).
Axes of the slice: x: 2, y: 2, z: 4, core: 2. Of those that a mesh axis runs over, the one named last changes fastest.
Arguments:
- pilots: bfloat16 [128, 1024, 1024], P(('region', 'cluster')), may hold values from -0.1875 to 0.1875
- estimate: bfloat16 [128, 8, 1024], P(('region', 'cluster')), may hold values from -6 to 6
- visible: int32 [128, 1024], P(('region', 'cluster')), may hold values from 0 to 65535, as said below
- blocks: int32 [128], P(('region', 'cluster')), may hold values from 4 to 8
- received: float32 [128, 8, 1024], P(('region', 'cluster')), may hold values from -6 to 6
- previous: float32 [128, 8, 1024], P(('region', 'cluster')), may hold values from -6 to 6
- onsager: float32 [128], P(('region', 'cluster')), may hold values from 0.2 to 0.8
- user_cluster: int32 [65536], replicated, may hold values from 0 to 15
- cluster_prior: float32 [16], replicated, may hold values from -4 to 0
Outputs:
- new_estimate: bfloat16 [128, 8, 1024], P(('region', 'cluster'))
- residual: float32 [128, 8, 1024], P(('region', 'cluster'))
- posterior: float32 [65536], P(('region', 'cluster'))
Inputs may be any that keep to these rules, and one draw needn't show every extreme that they name: Every draw has some access point with 8 live blocks. `visible`: users are numbered region by region, 2048 * 8 to a region, in the order of the devices along region+cluster. An access point hears only users of its own region or of the two regions beside it along region (the first and the last region are beside each other); most of the users it hears are of its own region.
All inputs are finite; a program needn't handle non-finite values.
Results may differ from a plain program's by a relative error of at most 0.0056.
Values sent between devices are 32-bit elements; how exact they have to be, the bound alone decides.
A program may use at most 192 MiB of HBM per device.

v0:
```python
import jax
import jax.numpy as jnp
from jax import lax
from jax.sharding import PartitionSpec as P

ROW_BLOCK = 128
U_DEV = 2048


epsilon = 1e-06


def passed_along(block, axis, distance):
    devices = range(lax.axis_size(axis))
    route = [((i - distance) % len(devices), i) for i in devices]
    return lax.ppermute(block, axis, route)


def decide(summed, start, count, user_cluster, cluster_prior):
    labels = lax.dynamic_slice_in_dim(user_cluster, start, count)
    table = jnp.arange(cluster_prior.shape[0], dtype=jnp.int32)
    prior = jnp.sum(
        jnp.where(labels[:, None] == table[None, :], cluster_prior[None, :], jnp.float32(0.0)),
        axis=1,
    )
    return jax.nn.sigmoid(summed + prior)


def local(
    pilots, estimate, visible, blocks, received, previous, onsager, user_cluster, cluster_prior
):
    points, antennas, slots = estimate.shape
    live = jnp.arange(slots)[None, :] // ROW_BLOCK < blocks[:, None]
    masked = jnp.where(live[:, None, :], estimate, jnp.zeros_like(estimate))
    widened = masked.astype(jnp.float32)
    product = jnp.einsum("amr,arl->aml", masked, pilots, preferred_element_type=jnp.float32)
    resid = received - product + onsager[:, None, None] * previous
    spread = jnp.mean(resid * resid, axis=(1, 2)) + epsilon
    narrow = resid.astype(jnp.bfloat16)
    stat = widened + jnp.einsum("aml,arl->amr", narrow, pilots, preferred_element_type=jnp.float32)
    energy = jnp.sum(stat * stat, axis=1)
    base = 0.5 * antennas * jnp.log(spread / (1.0 + spread))
    llr = base[:, None] + energy / (2.0 * spread * (1.0 + spread))[:, None]
    llr = jnp.where(live, llr, jnp.float32(0.0))
    total_users = U_DEV * lax.axis_size("region") * lax.axis_size("cluster")
    own_start = lax.axis_index(("region", "cluster")) * U_DEV
    flat_llr = llr.reshape(-1)
    region_users = U_DEV * lax.axis_size("cluster")
    regions = lax.axis_size("region")
    lowest = (lax.axis_index("region") + regions - 1) % regions * region_users
    relative = (visible - lowest + total_users) % total_users
    window = jax.ops.segment_sum(flat_llr, relative.reshape(-1), num_segments=3 * region_users)
    from_below = passed_along(window[2 * region_users :], "region", 1)
    from_above = passed_along(window[:region_users], "region", -1)
    region_sum = window[region_users : 2 * region_users] + from_below + from_above
    owned_sum = lax.psum_scatter(region_sum, "cluster", scatter_dimension=0, tiled=True)
    owned = decide(owned_sum, own_start, U_DEV, user_cluster, cluster_prior)
    own_post = lax.all_gather(owned, "cluster", axis=0, tiled=True)
    below = passed_along(own_post, "region", 1)
    above = passed_along(own_post, "region", -1)
    nearby = jnp.concatenate([below, own_post, above])
    rate = nearby[relative]
    fresh = rate[:, None, :] * stat / (1.0 + spread)[:, None, None]
    new_estimate = jnp.where(live[:, None, :], fresh, jnp.float32(0.0)).astype(jnp.bfloat16)
    return (new_estimate, resid, owned)


def solution(mesh):
    placed = (
        P(("region", "cluster"), None, None),
        P(("region", "cluster"), None, None),
        P(("region", "cluster"), None),
        P(("region", "cluster")),
        P(("region", "cluster"), None, None),
        P(("region", "cluster"), None, None),
        P(("region", "cluster")),
        P(),
        P(),
    )
    return jax.shard_map(
        local,
        mesh=mesh,
        in_specs=placed,
        out_specs=(
            P(("region", "cluster"), None, None),
            P(("region", "cluster"), None, None),
            P(("region", "cluster")),
        ),
        check_vma=False,
    )
```

profile of v0, /device:TPU:1, one launch (start us, length us, event | category | flops | bytes accessed | tf_op | source)
XLA Modules:
  0.0 152.7 jit_solution(528623752502533669)
XLA Ops:
  7.2 0.0 copy-start.2
  7.2 0.0 all-reduce.3.cloned.1.call-start
  7.3 0.0 copy-start
  7.3 0.9 fusion.7
  8.2 0.9 broadcast_compare_fusion
  9.1 0.0 copy-start.6
  9.1 5.3 %multiply_reduce_fusion.1 = (f32[4]{0:T(128)S(1)}, f32[4,8,1024]{2,1,0:T(8,128)S(1)}) fusion(f32[4,8,1024]{2,1,0:T(8,128)} %param.14, f32[4]{0:T(128)} %param.15, f32[4,8,1024]{2,1,0:T(8,128)} %param.13, bf16[4,1024,1024]{2,1,0:T(8,128)(2,1)} %param.9, bf16[4,8,1024]{2,1,0:T(8,128)(2,1)} %param.10, pred[4,1024]{1,0:T(4,128)(4,1)S(1)} %broadcast_compare_fusion), kind=kOutput, calls=%fused_computation.10 | convolution fusion | flops 67305472 | bytes 8851488 | tf_op jit(solution)/shard_map/amr,arl->aml/dot_general | solution.py:36
  14.4 0.0 copy-done
  14.4 2.3 %multiply_reduce_fusion = (f32[4,1024]{1,0:T(4,128)S(1)}, f32[4,8,1024]{2,1,0:T(8,128)S(1)}) fusion(bf16[4,1024,1024]{2,1,0:T(8,128)(2,1)S(1)} %copy-done, f32[4,8,1024]{2,1,0:T(8,128)S(1)} %get-tuple-element.11, bf16[4,8,1024]{2,1,0:T(8,128)(2,1)S(1)} %copy-done.2, pred[4,1024]{1,0:T(4,128)(4,1)S(1)} %broadcast_compare_fusion), kind=kOutput, calls=%fused_computation.9 | convolution fusion | flops 67301376 | bytes 8736768 | tf_op jit(solution)/shard_map/aml,arl->amr/dot_general | solution.py:40
  16.7 0.1 select_bitcast_fusion
  16.8 21.9 %scatter_custom_fusion = f32[49152]{0:T(1024)S(1)} fusion(s32[4096]{0:T(1024)S(1)} %bitcast.17, f32[4096]{0:T(1024)S(1)} %bitcast.18, f32[]{:T(128)} %constant.68.clone.1), kind=kCustom, calls=%fused_computation.11 | custom fusion | flops 4096 | bytes 196612 | tf_op jit(solution)/shard_map/scatter-add | solution.py:52
  38.8 2.1 %collective-permute-start = (f32[16384]{0:T(1024)S(1)}, f32[16384]{0:T(1024)S(1)}, u32[]{:S(2)}, u32[]{:S(2)}) collective-permute-start(f32[16384]{0:T(1024)S(1)} %get-tuple-element.3), channel_id=1, source_target_pairs={{24,0},{0,8},{8,16},{16,24},{25,1},{1,9},{9,17},{17,25},{26,2},{2,... | collective-permute-start | bytes 196616 | tf_op jit(solution)/shard_map/ppermute | solution.py:16
  40.9 1.0 collective-permute-start.1
  41.9 0.7 dynamic_slice.3
  42.6 0.9 collective-permute-done
  43.5 1.3 collective-permute-done.1
  44.8 0.6 fusion.3
  45.4 0.0 all-reduce.3.cloned.1.call-update
  45.5 0.1 select_reduce_fusion
  45.6 0.0 copy-done.6
  45.6 0.6 dynamic-slice
  46.8 52.7 %all-reduce.3.cloned.1.call-done = f32[16384]{0:T(1024)} async-done(((f32[16384]{0:T(1024)}), f32[16384]{0:T(1024)}) %all-reduce.3.cloned.1.call-update) | async-done | bytes 65552
  99.5 0.7 fusion.11
  100.2 16.1 %all_gather.3 = f32[16384]{0:T(1024)S(1)} all-gather(f32[2048]{0:T(1024)S(1)} %fusion.11), channel_id=1, replica_groups=mesh['region'=4,'cluster'=8] {'cluster'}, dimensions={0}, use_global_device_ids=true | all-gather | bytes 73728 | tf_op jit(solution)/shard_map/all_gather | solution.py:58
  116.2 1.2 collective-permute-start.2
  117.4 1.2 collective-permute-start.3
  118.6 2.0 %collective-permute-done.2 = f32[16384]{0:T(1024)S(1)} collective-permute-done((f32[16384]{0:T(1024)S(1)}, f32[16384]{0:T(1024)S(1)}, u32[]{:S(2)}, u32[]{:S(2)}) %collective-permute-start.2) | collective-permute-done | bytes 65568 | tf_op jit(solution)/shard_map/ppermute | solution.py:16
  120.7 1.4 collective-permute-done.3
  122.1 23.0 %gather_fusion = f32[4096]{0:T(1024)S(1)} fusion(f32[49152]{0:T(1024)S(1)} %pad_maximum_fusion, s32[4096]{0:T(1024)S(1)} %bitcast_clamp_fusion), kind=kCustom, calls=%fused_computation | custom fusion | bytes 49152 | tf_op jit(solution)/shard_map/gather | solution.py:62
  145.1 0.0 copy-done.1
  145.1 0.0 copy-done.3
  145.2 0.7 select_convert_fusion
  (15 shorter events, 0.1 us)
Async XLA Ops:
  7.2 7.2 %copy-start.2 = (bf16[4,8,1024]{2,1,0:T(8,128)(2,1)S(1)}, bf16[4,8,1024]{2,1,0:T(8,128)(2,1)}, u32[]{:S(2)}) copy-start(bf16[4,8,1024]{2,1,0:T(8,128)(2,1)} %param.10) | copy-start | bytes 196612
  7.2 92.3 %all-reduce.3.cloned.1.call-start = ((), (), s32[]{:S(2)}) async-start(), calls=%async_computation | async-start | bytes 131072
  7.3 7.1 %copy-start = (bf16[4,1024,1024]{2,1,0:T(8,128)(2,1)S(1)}, bf16[4,1024,1024]{2,1,0:T(8,128)(2,1)}, u32[]{:S(2)}) copy-start(bf16[4,1024,1024]{2,1,0:T(8,128)(2,1)} %param.9) | copy-start | bytes 25165828
  9.1 7.7 %copy-start.4 = (s32[4]{0:T(128)S(1)}, s32[4]{0:T(128)}, u32[]{:S(2)}) copy-start(s32[4]{0:T(128)} %param.12) | copy-start | bytes 52
  9.1 36.4 %copy-start.5 = (f32[16]{0:T(128)S(1)}, f32[16]{0:T(128)}, u32[]{:S(2)}) copy-start(f32[16]{0:T(128)} %param.17) | copy-start | bytes 196
  9.1 36.5 %copy-start.6 = (u32[32]{0:T(128)S(1)}, u32[32]{0:T(128)}, u32[]{:S(2)}) copy-start(u32[32]{0:T(128)} %constant.94) | copy-start | bytes 388
  14.4 130.7 %copy-start.1 = (f32[4,8,1024]{2,1,0:T(8,128)}, f32[4,8,1024]{2,1,0:T(8,128)S(1)}, u32[]{:S(2)}) copy-start(f32[4,8,1024]{2,1,0:T(8,128)S(1)} %get-tuple-element.11) | copy-start | bytes 393220
  38.8 4.7 %collective-permute-start = (f32[16384]{0:T(1024)S(1)}, f32[16384]{0:T(1024)S(1)}, u32[]{:S(2)}, u32[]{:S(2)}) collective-permute-start(f32[16384]{0:T(1024)S(1)} %get-tuple-element.3), channel_id=1, source_target_pairs={{24,0},{0,8},{8,16},{16,24},{25,1},{1,9},{9,17},{17,25},{26,2},{2,... | collective-permute-start | bytes 196616 | tf_op jit(solution)/shard_map/ppermute | solution.py:16
  40.9 3.9 %collective-permute-start.1 = (f32[16384]{0:T(1024)S(1)}, f32[16384]{0:T(1024)S(1)}, u32[]{:S(2)}, u32[]{:S(2)}) collective-permute-start(f32[16384]{0:T(1024)S(1)} %get-tuple-element.4), channel_id=1, source_target_pairs={{8,0},{16,8},{24,16},{0,24},{9,1},{17,9},{25,17},{1,25},{10,2},{18... | collective-permute-start | bytes 196616 | tf_op jit(solution)/shard_map/ppermute | solution.py:16
  100.2 45.0 %copy-start.3 = (f32[2048]{0:T(1024)}, f32[2048]{0:T(1024)S(1)}, u32[]{:S(2)}) copy-start(f32[2048]{0:T(1024)S(1)} %fusion.11) | copy-start | bytes 24580
  116.2 4.4 %collective-permute-start.2 = (f32[16384]{0:T(1024)S(1)}, f32[16384]{0:T(1024)S(1)}, u32[]{:S(2)}, u32[]{:S(2)}) collective-permute-start(f32[16384]{0:T(1024)S(1)} %all_gather.3), channel_id=1, source_target_pairs={{24,0},{0,8},{8,16},{16,24},{25,1},{1,9},{9,17},{17,25},{26,2},{2,... | collective-permute-start | bytes 196616 | tf_op jit(solution)/shard_map/ppermute | solution.py:16
  117.4 4.6 %collective-permute-start.3 = (f32[16384]{0:T(1024)S(1)}, f32[16384]{0:T(1024)S(1)}, u32[]{:S(2)}, u32[]{:S(2)}) collective-permute-start(f32[16384]{0:T(1024)S(1)} %all_gather.3), channel_id=1, source_target_pairs={{8,0},{16,8},{24,16},{0,24},{9,1},{17,9},{25,17},{1,25},{10,2},{18... | collective-permute-start | bytes 196616 | tf_op jit(solution)/shard_map/ppermute | solution.py:16
Sparse Core Ops, SparseCore 0:
  45.6 53.8 all-reduce.2
where the time goes:
time: 154 us; the launch traced here: 153 us
  waiting for transfers between devices  58.3 us (38%)
  other arithmetic  26 us (17%)
  local copies, waits for them, and re-layouts  24.4 us (16%)
  blocking collectives  16.1 us (10%)
  between operations  14.9 us (10%)
  matrix products  7.59 us (5%)
  starting transfers between devices  5.52 us (4%)
    unnamed x2, waiting for transfers between devices  52.7 us
    gather x2, local copies, waits for them, and re-layouts, local(): rate = nearby[relative]  23 us
    scatter-add x1, other arithmetic, local(): jax.ops.segment_sum(flat_llr, relative.reshape(-1), num_segments=3 * regi...  21.9 us
    all_gather x1, blocking collectives, local(): own_post = lax.all_gather(owned, 'cluster', axis=0, tiled=True)  16.1 us
    ppermute x4, waiting for transfers between devices, passed_along(): return lax.ppermute(block, axis, route)  5.64 us
    ppermute x4, starting transfers between devices, passed_along(): return lax.ppermute(block, axis, route)  5.48 us
    dot_general x1, matrix products, local(): jnp.einsum('amr,arl->aml', masked, pilots, preferred_element_type=jnp.flo...  5.3 us
  transfers between devices with their start and end apart: 5, of which 5 were waited for; matrix products, arithmetic and copies ran while one was open for 1% of the time, Pallas kernels for 0%

commit v1 on v0

v1 whole, which is shorter than its diff:
```python
import functools

import jax
import jax.numpy as jnp
from jax import lax
from jax.experimental import pallas as pl
from jax.experimental.pallas import tpu as pltpu
from jax.sharding import PartitionSpec as P

ROW_BLOCK = 128
LANES = 128
TILE = 384
VMEM_LIMIT = 48 * 1024 * 1024
MESH = pl.DeviceIdType.MESH

epsilon = 1e-06


def halves(value):
    high = value.astype(jnp.bfloat16)
    low = (value - high.astype(jnp.float32)).astype(jnp.bfloat16)
    return high, low


def relative_ids(visible, users):
    regions = lax.axis_size("region")
    lowest = lax.rem(lax.axis_index("region") + (regions - 1), regions) * (users // regions)
    shifted = visible - lowest
    shifted = jnp.where(shifted < 0, shifted + users, shifted)
    return shifted // LANES, shifted % LANES


def one_hot(row, count, start=0):
    place = lax.broadcasted_iota(jnp.int32, (count, row.shape[1]), 0) + start
    return place == row


def statistics_kernel(
    users, blocks_ref, onsager_ref, pilots_ref, estimate_ref, visible_ref, received_ref,
    previous_ref, resid_ref, scaled_ref, window_ref,
):
    point = pl.program_id(0)
    antennas, slots = estimate_ref.shape[1:]
    slot = lax.broadcasted_iota(jnp.int32, (1, slots), 1)
    live = slot // ROW_BLOCK < blocks_ref[point]
    widened = jnp.where(live, estimate_ref[0].astype(jnp.float32), 0.0)
    masked = widened.astype(jnp.bfloat16)
    pilots = pilots_ref[0]
    product = jnp.dot(masked, pilots, preferred_element_type=jnp.float32)
    resid = received_ref[0] - product + onsager_ref[point] * previous_ref[0]
    resid_ref[0] = resid
    square = jnp.sum(jnp.sum(resid * resid, axis=0, keepdims=True), axis=1, keepdims=True)
    spread = square / (antennas * resid.shape[1]) + epsilon
    narrow = resid.astype(jnp.bfloat16)
    stat = widened + lax.dot_general(
        narrow, pilots, (((1,), (1,)), ((), ())), preferred_element_type=jnp.float32
    )
    energy = jnp.sum(stat * stat, axis=0, keepdims=True)
    base = 0.5 * antennas * jnp.log(spread / (1.0 + spread))
    llr = jnp.where(live, base + energy / (2.0 * spread * (1.0 + spread)), 0.0)
    scaled_ref[0] = jnp.where(live, stat / (1.0 + spread), 0.0)
    high_id, low_id = relative_ids(visible_ref[pl.ds(point, 1), :], users)
    high, low = halves(llr)
    lanes = one_hot(low_id, LANES)
    spread_out = jnp.concatenate(
        [
            jnp.where(lanes, high.astype(jnp.float32), 0.0).astype(jnp.bfloat16),
            jnp.where(lanes, low.astype(jnp.float32), 0.0).astype(jnp.bfloat16),
        ],
        axis=0,
    )
    for start in range(0, window_ref.shape[0], TILE):
        rows = jnp.where(one_hot(high_id, TILE, start), 1.0, 0.0).astype(jnp.bfloat16)
        both = lax.dot_general(
            rows, spread_out, (((1,), (1,)), ((), ())), preferred_element_type=jnp.float32
        )
        part = both[:, :LANES] + both[:, LANES:]

        @pl.when(point == 0)
        def _():
            window_ref[pl.ds(start, TILE), :] = part

        @pl.when(point > 0)
        def _():
            window_ref[pl.ds(start, TILE), :] += part


def exchange_kernel(
    window_ref, labels_ref, prior_ref, owned_ref, nearby_ref, arrived, labels, label_sem,
    sum_send, sum_recv, post_send, post_recv,
):
    regions, clusters = lax.axis_size("region"), lax.axis_size("cluster")
    region, cluster = lax.axis_index("region"), lax.axis_index("cluster")
    rows = owned_ref.shape[0]
    peers = 3 * clusters
    home = clusters + cluster

    def peer(j):
        slot = lax.rem(home + j, peers)
        step = slot // clusters
        device = (lax.rem(region + step + (regions - 1), regions), lax.rem(slot, clusters))
        back = (2 - step) * clusters + cluster
        return slot, back, device

    def part(ref, slot):
        return ref.at[pl.ds(pl.multiple_of(slot * rows, rows), rows), :]

    def sum_copy(source, target, device):
        return pltpu.make_async_remote_copy(
            src_ref=part(window_ref, source), dst_ref=part(arrived, target),
            send_sem=sum_send.at[source], recv_sem=sum_recv.at[target],
            device_id=device, device_id_type=MESH,
        )

    def post_copy(source, target, device):
        return pltpu.make_async_remote_copy(
            src_ref=owned_ref, dst_ref=part(nearby_ref, target),
            send_sem=post_send.at[source], recv_sem=post_recv.at[target],
            device_id=device, device_id_type=MESH,
        )

    own_rows = pl.ds(pl.multiple_of((region * clusters + cluster) * rows, rows), rows)
    fetch = pltpu.make_async_copy(labels_ref.at[own_rows, :], labels, label_sem)
    fetch.start()
    barrier = pltpu.get_barrier_semaphore()

    @pl.loop(1, peers)
    def _(j):
        _, _, device = peer(j)
        pl.semaphore_signal(barrier, inc=1, device_id=device, device_id_type=MESH)

    pl.semaphore_wait(barrier, peers - 1)

    @pl.loop(1, peers)
    def _(j):
        slot, back, device = peer(j)
        sum_copy(slot, back, device).start()

    fetch.wait()
    total = jnp.zeros(owned_ref.shape, jnp.float32)
    for k in range(prior_ref.shape[0]):
        total = total + jnp.where(labels[...] == k, prior_ref[k], 0.0)
    total = total + window_ref[pl.ds(pl.multiple_of(home * rows, rows), rows), :]

    def collect(j, total):
        slot, back, device = peer(j)
        sum_copy(slot, slot, device).wait_recv()
        return total + arrived[pl.ds(pl.multiple_of(slot * rows, rows), rows), :]

    total = lax.fori_loop(1, peers, collect, total)
    posterior = jax.nn.sigmoid(total)
    owned_ref[...] = posterior
    nearby_ref[pl.ds(pl.multiple_of(home * rows, rows), rows), :] = posterior

    @pl.loop(1, peers)
    def _(j):
        slot, back, device = peer(j)
        post_copy(slot, back, device).start()

    @pl.loop(1, peers)
    def _(j):
        slot, back, device = peer(j)
        post_copy(slot, slot, device).wait_recv()

    @pl.loop(1, peers)
    def _(j):
        slot, back, device = peer(j)
        sum_copy(slot, back, device).wait_send()
        post_copy(slot, back, device).wait_send()


def denoise_kernel(users, visible_ref, scaled_ref, nearby_ref, fresh_ref):
    table = jnp.concatenate(halves(nearby_ref[...]), axis=1)
    for point in range(visible_ref.shape[0]):
        high_id, low_id = relative_ids(visible_ref[pl.ds(point, 1), :], users)
        picked = None
        for start in range(0, nearby_ref.shape[0], TILE):
            rows = jnp.where(one_hot(high_id, TILE, start), 1.0, 0.0).astype(jnp.bfloat16)
            term = lax.dot_general(
                table[start : start + TILE], rows, (((0,), (0,)), ((), ())),
                preferred_element_type=jnp.float32,
            )
            picked = term if picked is None else picked + term
        picked = picked[:LANES] + picked[LANES:]
        rate = jnp.sum(jnp.where(one_hot(low_id, LANES), picked, 0.0), axis=0, keepdims=True)
        fresh_ref[point] = (rate * scaled_ref[point]).astype(jnp.bfloat16)


def local(
    pilots, estimate, visible, blocks, received, previous, onsager, user_cluster, cluster_prior
):
    points, antennas, slots = estimate.shape
    length = pilots.shape[2]
    users = user_cluster.shape[0]
    regions, clusters = lax.axis_size("region"), lax.axis_size("cluster")
    rows = users // (regions * clusters) // LANES
    window_rows = 3 * clusters * rows
    f32 = jnp.float32
    smem = pl.BlockSpec(memory_space=pltpu.SMEM)
    vmem = pl.BlockSpec(memory_space=pltpu.VMEM)
    each = lambda *shape: pl.BlockSpec((1,) + shape, lambda i: (i, 0, 0))
    whole = lambda *shape: pl.BlockSpec(shape, lambda i: (0, 0))
    resid, scaled, window = pl.pallas_call(
        functools.partial(statistics_kernel, users),
        grid=(points,),
        in_specs=[
            smem, smem, each(slots, length), each(antennas, slots), whole(points, slots),
            each(antennas, length), each(antennas, length),
        ],
        out_specs=[each(antennas, length), each(antennas, slots), whole(window_rows, LANES)],
        out_shape=[
            jax.ShapeDtypeStruct((points, antennas, length), f32),
            jax.ShapeDtypeStruct((points, antennas, slots), f32),
            jax.ShapeDtypeStruct((window_rows, LANES), f32),
        ],
        compiler_params=pltpu.CompilerParams(vmem_limit_bytes=VMEM_LIMIT),
    )(blocks, onsager, pilots, estimate, visible, received, previous)
    peers = 3 * clusters
    owned, nearby = pl.pallas_call(
        exchange_kernel,
        in_specs=[vmem, pl.BlockSpec(memory_space=pl.ANY), smem],
        out_specs=[vmem, vmem],
        out_shape=[
            jax.ShapeDtypeStruct((rows, LANES), f32),
            jax.ShapeDtypeStruct((window_rows, LANES), f32),
        ],
        scratch_shapes=[
            pltpu.VMEM((window_rows, LANES), f32),
            pltpu.VMEM((rows, LANES), jnp.int32),
            pltpu.SemaphoreType.DMA,
        ]
        + [pltpu.SemaphoreType.DMA((peers,))] * 4,
        compiler_params=pltpu.CompilerParams(collective_id=0, has_side_effects=True),
    )(window, user_cluster.reshape(-1, LANES), cluster_prior)
    new_estimate = pl.pallas_call(
        functools.partial(denoise_kernel, users),
        in_specs=[vmem, vmem, vmem],
        out_specs=vmem,
        out_shape=jax.ShapeDtypeStruct((points, antennas, slots), jnp.bfloat16),
        compiler_params=pltpu.CompilerParams(vmem_limit_bytes=VMEM_LIMIT),
    )(visible, scaled, nearby)
    return (new_estimate, resid, owned.reshape(-1))


def solution(mesh):
    device = ("region", "cluster")
    placed = (
        P(device, None, None),
        P(device, None, None),
        P(device, None),
        P(device),
        P(device, None, None),
        P(device, None, None),
        P(device),
        P(),
        P(),
    )
    return jax.shard_map(
        local,
        mesh=mesh,
        in_specs=placed,
        out_specs=(P(device, None, None), P(device, None, None), P(device)),
        check_vma=False,
    )
```

time: 154 us -> 41.1 us (0.27)
  waiting for transfers between devices: 58.3 us -> 0 us
  Pallas kernels: 0 us -> 32.1 us
  other arithmetic: 26 us -> 0 us
  local copies, waits for them, and re-layouts: 24.4 us -> 7.56 us
  blocking collectives: 16.1 us -> 0 us
  between operations: 14.9 us -> 0.67 us
  matrix products: 7.59 us -> 0 us
  starting transfers between devices: 5.52 us -> 0 us
    unnamed x2 -> x0, waiting for transfers between devices: 52.7 us -> none
    pallas_call x0 -> x3, Pallas kernels: none -> 32.1 us  [the longest x1 21.9 us: local(): pl.pallas_call(exchange_kernel, in_specs=[vmem, pl.BlockSpec(memory_space...]
    gather x2 -> x0, local copies, waits for them, and re-layouts: 23 us -> none  [local(): rate = nearby[relative]]
    scatter-add x1 -> x0, other arithmetic: 21.9 us -> none  [local(): jax.ops.segment_sum(flat_llr, relative.reshape(-1), num_segments=3 * regi...]
    all_gather x1 -> x0, blocking collectives: 16.1 us -> none  [local(): own_post = lax.all_gather(owned, 'cluster', axis=0, tiled=True)]
    dot_general x2 -> x0, matrix products: 7.59 us -> none  [the longest x1 5.3 us: local(): jnp.einsum('amr,arl->aml', masked, pilots, preferred_element_type=jnp.flo...]
    unnamed x17 -> x19, local copies, waits for them, and re-layouts: 0.63 us -> 7.56 us
    ppermute x4 -> x0, waiting for transfers between devices: 5.64 us -> none  [passed_along(): return lax.ppermute(block, axis, route)]
  transfers between devices with their start and end apart: 5 -> 0, of which waited for: 5 -> 0; matrix products, arithmetic and copies ran while one was open for 1% -> 0% of each run, Pallas kernels for 0% -> 0%
where the time goes in v1:
time: 41.1 us; the launch traced here: 40.3 us
  Pallas kernels  32.1 us (78%)
  local copies, waits for them, and re-layouts  7.56 us (18%)
  between operations  0.67 us (2%)
    pallas_call x1, Pallas kernels, local(): pl.pallas_call(exchange_kernel, in_specs=[vmem, pl.BlockSpec(memory_space...  21.9 us
    pallas_call x1, Pallas kernels, local(): pl.pallas_call(functools.partial(statistics_kernel, users), grid=(points,...  7.76 us
    unnamed x19, local copies, waits for them, and re-layouts  7.56 us
    pallas_call x1, Pallas kernels, local(): pl.pallas_call(functools.partial(denoise_kernel, users), in_specs=[vmem,...  2.43 us

profile of v1, /device:TPU:1, one launch (start us, length us, event | category | flops | bytes accessed | tf_op | source)
XLA Modules:
  0.0 40.3 jit_solution(4177304349792031328)
XLA Ops:
  0.6 0.0 copy-start.2
  0.6 0.9 %copy-done.2 = f32[4,8,1024]{2,1,0:T(8,128)S(1)} copy-done((f32[4,8,1024]{2,1,0:T(8,128)S(1)}, f32[4,8,1024]{2,1,0:T(8,128)}, u32[]{:S(2)}) %copy-start.2) | copy-done | bytes 131096
  1.5 0.0 copy-start.3
  1.5 0.9 %copy-done.3 = f32[4,8,1024]{2,1,0:T(8,128)S(1)} copy-done((f32[4,8,1024]{2,1,0:T(8,128)S(1)}, f32[4,8,1024]{2,1,0:T(8,128)}, u32[]{:S(2)}) %copy-start.3) | copy-done | bytes 131096
  2.4 0.0 copy-start.4
  2.4 0.8 %copy-done.4 = bf16[4,8,1024]{2,1,0:T(8,128)(2,1)S(1)} copy-done((bf16[4,8,1024]{2,1,0:T(8,128)(2,1)S(1)}, bf16[4,8,1024]{2,1,0:T(8,128)(2,1)}, u32[]{:S(2)}) %copy-start.4) | copy-done | bytes 65560
  3.3 0.0 copy-start.5
  3.3 0.7 %copy-done.5 = s32[4,1024]{1,0:T(4,128)S(1)} copy-done((s32[4,1024]{1,0:T(4,128)S(1)}, s32[4,1024]{1,0:T(4,128)}, u32[]{:S(2)}) %copy-start.5) | copy-done | bytes 16408
  4.0 0.0 copy-start.7
  4.0 0.7 %copy-done.7 = s32[4]{0:T(128)S(1)} copy-done((s32[4]{0:T(128)S(1)}, s32[4]{0:T(128)}, u32[]{:S(2)}) %copy-start.7) | copy-done | bytes 40
  4.7 0.0 copy-start.8
  4.7 0.7 %copy-done.8 = f32[4]{0:T(128)S(1)} copy-done((f32[4]{0:T(128)S(1)}, f32[4]{0:T(128)}, u32[]{:S(2)}) %copy-start.8) | copy-done | bytes 40
  5.3 0.0 copy-start.6
  5.3 7.8 %shard_map.112 = (f32[4,8,1024]{2,1,0:T(8,128)}, f32[4,8,1024]{2,1,0:T(8,128)S(1)}, f32[384,128]{1,0:T(8,128)S(1)}) custom-call(s32[4]{0:T(128)S(1)} %copy-done.7, f32[4]{0:T(128)S(1)} %copy-done.8, bf16[4,1024,1024]{2,1,0:T(8,128)(2,1)} %pilots_ref.1, bf16[4,8,1024]{2,1,0:T(8,128)(2,1)S(1)} %copy-done.4, s32[4,1024]{1,0:T(4,128)S(1)} %copy-done.5, ...), custom_call_target="tpu_custom_call" | custom-call | tf_op jit(solution)/shard_map/pallas_call | solution.py:203
  13.1 0.0 copy-start
  13.1 0.7 %copy-done = f32[384,128]{1,0:T(8,128)} copy-done((f32[384,128]{1,0:T(8,128)}, f32[384,128]{1,0:T(8,128)S(1)}, u32[]{:S(2)}) %copy-start) | copy-done | bytes 196632
  13.8 21.9 %shard_map.113 = (f32[16,128]{1,0:T(8,128)}, f32[384,128]{1,0:T(8,128)}) custom-call(f32[384,128]{1,0:T(8,128)} %copy-done, s32[512,128]{1,0:T(8,128)} %bitcast.2, f32[16]{0:T(128)} %prior_ref.1), custom_call_target="tpu_custom_call" | custom-call | tf_op jit(solution)/shard_map/pallas_call | solution.py:219
  35.7 0.0 copy-done.6
  35.7 0.0 copy-start.1
  35.7 0.9 %copy-done.1 = f32[384,128]{1,0:T(8,128)S(1)} copy-done((f32[384,128]{1,0:T(8,128)S(1)}, f32[384,128]{1,0:T(8,128)}, u32[]{:S(2)}) %copy-start.1) | copy-done | bytes 196632
  36.6 2.4 %shard_map.114 = bf16[4,8,1024]{2,1,0:T(8,128)(2,1)} custom-call(s32[4,1024]{1,0:T(4,128)S(1)} %copy-done.6, f32[4,8,1024]{2,1,0:T(8,128)S(1)} %get-tuple-element.8.scaled_ref, f32[384,128]{1,0:T(8,128)S(1)} %copy-done.1), custom_call_target="tpu_custom_call" | custom-call | tf_op jit(solution)/shard_map/pallas_call | solution.py:235
  39.1 1.3 %copy.13 = f32[2048]{0:T(1024)} copy(f32[2048]{0:T(1024)} %bitcast.3) | data formatting | bytes 16384
Async XLA Ops:
  0.6 0.9 %copy-start.2 = (f32[4,8,1024]{2,1,0:T(8,128)S(1)}, f32[4,8,1024]{2,1,0:T(8,128)}, u32[]{:S(2)}) copy-start(f32[4,8,1024]{2,1,0:T(8,128)} %received_ref.1) | copy-start | bytes 393220
  1.5 0.9 %copy-start.3 = (f32[4,8,1024]{2,1,0:T(8,128)S(1)}, f32[4,8,1024]{2,1,0:T(8,128)}, u32[]{:S(2)}) copy-start(f32[4,8,1024]{2,1,0:T(8,128)} %previous_ref.1) | copy-start | bytes 393220
  2.4 0.8 %copy-start.4 = (bf16[4,8,1024]{2,1,0:T(8,128)(2,1)S(1)}, bf16[4,8,1024]{2,1,0:T(8,128)(2,1)}, u32[]{:S(2)}) copy-start(bf16[4,8,1024]{2,1,0:T(8,128)(2,1)} %estimate_ref.1) | copy-start | bytes 196612
  3.3 0.7 %copy-start.5 = (s32[4,1024]{1,0:T(4,128)S(1)}, s32[4,1024]{1,0:T(4,128)}, u32[]{:S(2)}) copy-start(s32[4,1024]{1,0:T(4,128)} %visible_ref.3) | copy-start | bytes 49156
  4.0 0.7 %copy-start.7 = (s32[4]{0:T(128)S(1)}, s32[4]{0:T(128)}, u32[]{:S(2)}) copy-start(s32[4]{0:T(128)} %blocks_ref.1) | copy-start | bytes 52
  4.7 0.7 %copy-start.8 = (f32[4]{0:T(128)S(1)}, f32[4]{0:T(128)}, u32[]{:S(2)}) copy-start(f32[4]{0:T(128)} %onsager_ref.1) | copy-start | bytes 52
  5.3 30.4 %copy-start.6 = (s32[4,1024]{1,0:T(4,128)S(1)}, s32[4,1024]{1,0:T(4,128)}, u32[]{:S(2)}) copy-start(s32[4,1024]{1,0:T(4,128)} %visible_ref.3) | copy-start | bytes 49156
  13.1 0.7 %copy-start = (f32[384,128]{1,0:T(8,128)}, f32[384,128]{1,0:T(8,128)S(1)}, u32[]{:S(2)}) copy-start(f32[384,128]{1,0:T(8,128)S(1)} %get-tuple-element.9.window_ref) | copy-start | bytes 589828
  35.7 0.9 %copy-start.1 = (f32[384,128]{1,0:T(8,128)S(1)}, f32[384,128]{1,0:T(8,128)}, u32[]{:S(2)}) copy-start(f32[384,128]{1,0:T(8,128)} %get-tuple-element.10.nearby_ref) | copy-start | bytes 589828

commit v2 on v0

v2 whole, which is shorter than its diff:
```python
import functools

import jax
import jax.numpy as jnp
from jax import lax
from jax.experimental import pallas as pl
from jax.experimental.pallas import tpu as pltpu
from jax.sharding import PartitionSpec as P

ROW_BLOCK = 128
LANES = 128
TILE = 384
VMEM_LIMIT = 60 * 1024 * 1024
MESH = pl.DeviceIdType.MESH

epsilon = 1e-06


def halves(value):
    high = value.astype(jnp.bfloat16)
    low = (value - high.astype(jnp.float32)).astype(jnp.bfloat16)
    return high, low


def window_places(visible, users, rows):
    regions, clusters = lax.axis_size("region"), lax.axis_size("cluster")
    lowest = lax.rem(lax.axis_index("region") + (regions - 1), regions) * (users // regions)
    shifted = visible - lowest
    shifted = jnp.where(shifted < 0, shifted + users, shifted)
    line = lax.div(shifted, LANES)
    device = lax.div(line, rows)
    place = lax.rem(device, 2) * (3 * clusters // 2) + lax.div(device, 2)
    return place * rows + lax.rem(line, rows), lax.rem(shifted, LANES)


def one_hot(row, count, start=0):
    place = lax.broadcasted_iota(jnp.int32, (count, row.shape[1]), 0) + start
    return place == row


def main_kernel(
    pilots_hbm, estimate_hbm, visible_hbm, blocks_hbm, received_hbm, previous_hbm, onsager_hbm,
    labels_hbm, prior_hbm,
    resid_hbm, scaled_hbm, nearby_hbm,
    pilots, estimate, visible, blocks, received, previous, onsager, labels, prior,
    resid_out, scaled, nearby, selector, window, swapped, half, arrived, owned,
    load_sem, pilot_sem, store_sem, swap_sem, sum_send, sum_recv, post_send, post_recv,
):
    regions, clusters = lax.axis_size("region"), lax.axis_size("cluster")
    region, cluster = lax.axis_index("region"), lax.axis_index("cluster")
    core, chip, chips = lax.rem(cluster, 2), lax.div(cluster, 2), clusters // 2
    points, antennas, slots = estimate.shape
    rows = owned.shape[0]
    users = labels_hbm.shape[0] * LANES
    peers = 3 * chips
    half_rows = peers * rows
    home = chips + chip
    partner = (region, cluster + 1 - 2 * core)

    def part(ref, slot):
        return ref.at[pl.ds(pl.multiple_of(slot * rows, rows), rows), :]

    def side(ref, which):
        return ref.at[pl.ds(pl.multiple_of(which * half_rows, half_rows), half_rows), :]

    own_rows = pl.ds(pl.multiple_of((region * clusters + cluster) * rows, rows), rows)
    loads = [
        pltpu.make_async_copy(source, target, load_sem.at[i])
        for i, (source, target) in enumerate(
            [
                (visible_hbm, visible), (blocks_hbm, blocks), (estimate_hbm, estimate),
                (onsager_hbm, onsager), (received_hbm, received), (previous_hbm, previous),
                (prior_hbm, prior), (labels_hbm.at[own_rows, :], labels),
            ]
        )
    ]
    fetches = [
        pltpu.make_async_copy(pilots_hbm.at[i], pilots.at[i], pilot_sem.at[i])
        for i in range(points)
    ]
    for copy in loads[:4]:
        copy.start()
    fetches[0].start()
    for copy in loads[4:]:
        copy.start()
    for copy in fetches[1:]:
        copy.start()

    def peer(j):
        slot = lax.rem(home + j, peers)
        step = slot // chips
        device = (
            lax.rem(region + step + (regions - 1), regions), lax.rem(slot, chips) * 2 + core
        )
        back = (2 - step) * chips + chip
        return slot, back, device

    barrier = pltpu.get_barrier_semaphore()
    pl.semaphore_signal(barrier, inc=1, device_id=partner, device_id_type=MESH)

    @pl.loop(1, peers)
    def _(j):
        _, _, device = peer(j)
        pl.semaphore_signal(barrier, inc=1, device_id=device, device_id_type=MESH)

    loads[0].wait()
    row_id, lane_id = window_places(visible[...], users, rows)
    for point in range(points):
        for start in range(0, 2 * half_rows, TILE):
            selector[pl.ds(start, TILE), pl.ds(point * slots, slots)] = jnp.where(
                one_hot(row_id[point : point + 1], TILE, start), 1.0, 0.0
            ).astype(jnp.bfloat16)
    for copy in loads[1:]:
        copy.wait()
    slot_block = lax.broadcasted_iota(jnp.int32, (1, slots), 1) // ROW_BLOCK
    for point in range(points):
        live = slot_block < blocks[0:1, point : point + 1]
        widened = jnp.where(live, estimate[point].astype(jnp.float32), 0.0)
        masked = widened.astype(jnp.bfloat16)
        fetches[point].wait()
        product = jnp.dot(masked, pilots[point], preferred_element_type=jnp.float32)
        resid = received[point] - product + onsager[0:1, point : point + 1] * previous[point]
        resid_out[point] = resid
        square = jnp.sum(jnp.sum(resid * resid, axis=0, keepdims=True), axis=1, keepdims=True)
        spread = square / (antennas * resid.shape[1]) + epsilon
        narrow = resid.astype(jnp.bfloat16)
        stat = widened + lax.dot_general(
            narrow, pilots[point], (((1,), (1,)), ((), ())), preferred_element_type=jnp.float32
        )
        energy = jnp.sum(stat * stat, axis=0, keepdims=True)
        base = 0.5 * antennas * jnp.log(spread / (1.0 + spread))
        llr = jnp.where(live, base + energy / (2.0 * spread * (1.0 + spread)), 0.0)
        scaled[point] = jnp.where(live, stat / (1.0 + spread), 0.0)
        high, low = halves(llr)
        lanes = one_hot(lane_id[point : point + 1], LANES)
        values = jnp.concatenate(
            [
                jnp.where(lanes, high.astype(jnp.float32), 0.0).astype(jnp.bfloat16),
                jnp.where(lanes, low.astype(jnp.float32), 0.0).astype(jnp.bfloat16),
            ],
            axis=0,
        )
        for start in range(0, 2 * half_rows, TILE):
            both = lax.dot_general(
                selector[pl.ds(start, TILE), pl.ds(point * slots, slots)], values,
                (((1,), (1,)), ((), ())), preferred_element_type=jnp.float32,
            )
            term = both[:, :LANES] + both[:, LANES:]
            if point == 0:
                window[pl.ds(start, TILE), :] = term
            else:
                window[pl.ds(start, TILE), :] += term

    pl.semaphore_wait(barrier, peers)

    def swap(source, target, i):
        return pltpu.make_async_remote_copy(
            src_ref=source, dst_ref=target, send_sem=swap_sem.at[2 * i],
            recv_sem=swap_sem.at[2 * i + 1], device_id=partner, device_id_type=MESH,
        )

    first = swap(side(window, 1 - core), swapped, 0)
    first.start()
    stores = [
        pltpu.make_async_copy(resid_out, resid_hbm, store_sem.at[0]),
        pltpu.make_async_copy(scaled, scaled_hbm, store_sem.at[1]),
    ]
    for copy in stores:
        copy.start()
    total = jnp.zeros(owned.shape, jnp.float32)
    for k in range(prior.shape[1]):
        total = total + jnp.where(labels[...] == k, prior[0:1, k : k + 1], 0.0)
    first.wait_recv()
    half[...] = side(window, core)[...] + swapped[...]

    def sum_copy(source, target, device):
        return pltpu.make_async_remote_copy(
            src_ref=part(half, source), dst_ref=part(arrived, target),
            send_sem=sum_send.at[source], recv_sem=sum_recv.at[target],
            device_id=device, device_id_type=MESH,
        )

    def post_copy(source, target, device):
        return pltpu.make_async_remote_copy(
            src_ref=owned, dst_ref=part(nearby, core * peers + target),
            send_sem=post_send.at[source], recv_sem=post_recv.at[target],
            device_id=device, device_id_type=MESH,
        )

    @pl.loop(1, peers)
    def _(j):
        slot, back, device = peer(j)
        sum_copy(slot, back, device).start()

    total = total + part(half, home)[...]

    def collect(j, total):
        slot, _, device = peer(j)
        sum_copy(slot, slot, device).wait_recv()
        return total + part(arrived, slot)[...]

    posterior = jax.nn.sigmoid(lax.fori_loop(1, peers, collect, total))
    owned[...] = posterior

    @pl.loop(1, peers)
    def _(j):
        slot, back, device = peer(j)
        post_copy(slot, back, device).start()

    part(nearby, core * peers + home)[...] = posterior

    @pl.loop(1, peers)
    def _(j):
        slot, _, device = peer(j)
        post_copy(slot, slot, device).wait_recv()

    last = swap(side(nearby, core), side(nearby, core), 1)
    last.start()
    waiting = pltpu.make_async_remote_copy(
        src_ref=side(nearby, core), dst_ref=side(nearby, 1 - core), send_sem=swap_sem.at[2],
        recv_sem=swap_sem.at[3], device_id=partner, device_id_type=MESH,
    )
    waiting.wait_recv()
    finish = pltpu.make_async_copy(nearby, nearby_hbm, store_sem.at[2])
    finish.start()

    @pl.loop(1, peers)
    def _(j):
        slot, back, device = peer(j)
        sum_copy(slot, back, device).wait_send()
        post_copy(slot, back, device).wait_send()

    first.wait_send()
    last.wait_send()
    for copy in stores:
        copy.wait()
    finish.wait()


def denoise_kernel(
    users, visible_hbm, scaled_hbm, nearby_hbm, resid_hbm, fresh_hbm, resid_out, owned_out,
    visible, scaled, nearby, fresh, sem, store_sem,
):
    clusters, cluster = lax.axis_size("cluster"), lax.axis_index("cluster")
    rows = owned_out.shape[0]
    points = visible.shape[0]
    place = lax.rem(cluster, 2) * (3 * clusters // 2) + clusters // 2 + lax.div(cluster, 2)
    own_rows = pl.ds(pl.multiple_of(place * rows, rows), rows)
    copies = [
        pltpu.make_async_copy(source, target, sem.at[i])
        for i, (source, target) in enumerate(
            [
                (visible_hbm, visible), (nearby_hbm, nearby), (scaled_hbm, scaled),
                (resid_hbm, resid_out), (nearby_hbm.at[own_rows, :], owned_out),
            ]
        )
    ]
    for copy in copies:
        copy.start()
    copies[0].wait()
    row_id, lane_id = window_places(visible[...], users, rows)
    copies[1].wait()
    table = jnp.concatenate(halves(nearby[...]), axis=1)
    copies[2].wait()
    stores = []
    for point in range(points):
        picked = None
        for start in range(0, nearby.shape[0], TILE):
            hot = jnp.where(one_hot(row_id[point : point + 1], TILE, start), 1.0, 0.0)
            term = lax.dot_general(
                table[start : start + TILE], hot.astype(jnp.bfloat16), (((0,), (0,)), ((), ())),
                preferred_element_type=jnp.float32,
            )
            picked = term if picked is None else picked + term
        picked = picked[:LANES] + picked[LANES:]
        lanes = one_hot(lane_id[point : point + 1], LANES)
        rate = jnp.sum(jnp.where(lanes, picked, 0.0), axis=0, keepdims=True)
        fresh[point] = (rate * scaled[point]).astype(jnp.bfloat16)
        stores.append(
            pltpu.make_async_copy(fresh.at[point], fresh_hbm.at[point], store_sem.at[point])
        )
        stores[-1].start()
    for copy in copies[3:] + stores:
        copy.wait()


def local(
    pilots, estimate, visible, blocks, received, previous, onsager, user_cluster, cluster_prior
):
    points, antennas, slots = estimate.shape
    length = pilots.shape[2]
    users = user_cluster.shape[0]
    regions, clusters = lax.axis_size("region"), lax.axis_size("cluster")
    rows = users // (regions * clusters) // LANES
    peers = 3 * clusters // 2
    half_rows = peers * rows
    f32, i32, bf16 = jnp.float32, jnp.int32, jnp.bfloat16
    place = pl.BlockSpec(memory_space=pl.ANY)
    shape, vmem, dma = jax.ShapeDtypeStruct, pltpu.VMEM, pltpu.SemaphoreType.DMA
    resid, scaled, nearby = pl.pallas_call(
        main_kernel,
        in_specs=[place] * 9,
        out_specs=[place] * 3,
        out_shape=[
            shape((points, antennas, length), f32),
            shape((points, antennas, slots), f32),
            shape((2 * half_rows, LANES), f32),
        ],
        scratch_shapes=[
            vmem((points, slots, length), bf16),
            vmem((points, antennas, slots), bf16),
            vmem((points, slots), i32),
            vmem((1, points), i32),
            vmem((points, antennas, length), f32),
            vmem((points, antennas, length), f32),
            vmem((1, points), f32),
            vmem((rows, LANES), i32),
            vmem((1, cluster_prior.shape[0]), f32),
            vmem((points, antennas, length), f32),
            vmem((points, antennas, slots), f32),
            vmem((2 * half_rows, LANES), f32),
            vmem((2 * half_rows, points * slots), bf16),
            vmem((2 * half_rows, LANES), f32),
            vmem((half_rows, LANES), f32),
            vmem((half_rows, LANES), f32),
            vmem((half_rows, LANES), f32),
            vmem((rows, LANES), f32),
            dma((8,)), dma((points,)), dma((3,)), dma((4,)),
            dma((peers,)), dma((peers,)), dma((peers,)), dma((peers,)),
        ],
        compiler_params=pltpu.CompilerParams(
            collective_id=0, has_side_effects=True, vmem_limit_bytes=VMEM_LIMIT
        ),
    )(
        pilots, estimate, visible, blocks.reshape(1, -1), received, previous,
        onsager.reshape(1, -1), user_cluster.reshape(-1, LANES), cluster_prior.reshape(1, -1),
    )
    new_estimate, resid, owned = pl.pallas_call(
        functools.partial(denoise_kernel, users),
        in_specs=[place] * 4,
        out_specs=[place] * 3,
        out_shape=[
            shape((points, antennas, slots), bf16),
            shape((points, antennas, length), f32),
            shape((rows, LANES), f32),
        ],
        scratch_shapes=[
            vmem((points, slots), i32),
            vmem((points, antennas, slots), f32),
            vmem((2 * half_rows, LANES), f32),
            vmem((points, antennas, slots), bf16),
            dma((5,)), dma((points,)),
        ],
        compiler_params=pltpu.CompilerParams(vmem_limit_bytes=VMEM_LIMIT),
    )(visible, scaled, nearby, resid)
    return (new_estimate, resid, owned.reshape(-1))


def solution(mesh):
    device = ("region", "cluster")
    placed = (
        P(device, None, None),
        P(device, None, None),
        P(device, None),
        P(device),
        P(device, None, None),
        P(device, None, None),
        P(device),
        P(),
        P(),
    )
    return jax.shard_map(
        local,
        mesh=mesh,
        in_specs=placed,
        out_specs=(P(device, None, None), P(device, None, None), P(device)),
        check_vma=False,
    )
```

time: 154 us -> 31.5 us (0.20)
  waiting for transfers between devices: 58.3 us -> 0 us
  Pallas kernels: 0 us -> 30.5 us
  other arithmetic: 26 us -> 0 us
  local copies, waits for them, and re-layouts: 24.4 us -> 0 us
  blocking collectives: 16.1 us -> 0 us
  between operations: 14.9 us -> 0.64 us
  matrix products: 7.59 us -> 0 us
  starting transfers between devices: 5.52 us -> 0 us
    unnamed x2 -> x0, waiting for transfers between devices: 52.7 us -> none
    pallas_call x0 -> x2, Pallas kernels: none -> 30.5 us  [the longest x1 25.1 us: local(): pl.pallas_call(main_kernel, in_specs=[place] * 9, out_specs=[place] * 3,...]
    gather x2 -> x0, local copies, waits for them, and re-layouts: 23 us -> none  [local(): rate = nearby[relative]]
    scatter-add x1 -> x0, other arithmetic: 21.9 us -> none  [local(): jax.ops.segment_sum(flat_llr, relative.reshape(-1), num_segments=3 * regi...]
    all_gather x1 -> x0, blocking collectives: 16.1 us -> none  [local(): own_post = lax.all_gather(owned, 'cluster', axis=0, tiled=True)]
    dot_general x2 -> x0, matrix products: 7.59 us -> none  [the longest x1 5.3 us: local(): jnp.einsum('amr,arl->aml', masked, pilots, preferred_element_type=jnp.flo...]
    ppermute x4 -> x0, waiting for transfers between devices: 5.64 us -> none  [passed_along(): return lax.ppermute(block, axis, route)]
    ppermute x4 -> x0, starting transfers between devices: 5.48 us -> none  [passed_along(): return lax.ppermute(block, axis, route)]
  transfers between devices with their start and end apart: 5 -> 0, of which waited for: 5 -> 0; matrix products, arithmetic and copies ran while one was open for 1% -> 0% of each run, Pallas kernels for 0% -> 0%
where the time goes in v2:
time: 31.5 us; the launch traced here: 31.1 us
  Pallas kernels  30.5 us (97%)
  between operations  0.64 us (2%)
    pallas_call x1, Pallas kernels, local(): pl.pallas_call(main_kernel, in_specs=[place] * 9, out_specs=[place] * 3,...  25.1 us
    pallas_call x1, Pallas kernels, local(): pl.pallas_call(functools.partial(denoise_kernel, users), in_specs=[place]...  5.42 us

profile of v2, /device:TPU:1, one launch (start us, length us, event | category | flops | bytes accessed | tf_op | source)
XLA Modules:
  0.0 31.1 jit_solution(15765949840438892544)
XLA Ops:
  0.6 25.1 %shard_map.112 = (f32[4,8,1024]{2,1,0:T(8,128)}, f32[4,8,1024]{2,1,0:T(8,128)}, f32[384,128]{1,0:T(8,128)}) custom-call(bf16[4,1024,1024]{2,1,0:T(8,128)(2,1)} %pilots_hbm.1, bf16[4,8,1024]{2,1,0:T(8,128)(2,1)} %estimate_hbm.1, s32[4,1024]{1,0:T(4,128)} %visible_hbm.3, s32[1,4]{1,0:T(1,128)} %bitcast.6, f32[4,8,1024]{2,1,0:T(8,128)} %received_hbm.1, ...), custom_call_target="tpu_custom_call" | custom-call | tf_op jit(solution)/shard_map/pallas_call | solution.py:300
  25.7 5.4 %shard_map.113 = (bf16[4,8,1024]{2,1,0:T(8,128)(2,1)}, f32[4,8,1024]{2,1,0:T(8,128)}, f32[16,128]{1,0:T(8,128)}) custom-call(s32[4,1024]{1,0:T(4,128)} %visible_hbm.3, f32[4,8,1024]{2,1,0:T(8,128)} %get-tuple-element.9.scaled_hbm, f32[384,128]{1,0:T(8,128)} %get-tuple-element.10.nearby_hbm, f32[4,8,1024]{2,1,0:T(8,128)} %get-tuple-element.11.resid_hbm), custom_call_target="tpu_custom_call" | custom-call | tf_op jit(solution)/shard_map/pallas_call | solution.py:338

commit v3 on v2

--- a/solution.py
+++ b/solution.py
@@ -1,5 +1,3 @@
-import functools
-
 import jax
 import jax.numpy as jnp
 from jax import lax
@@ -10,7 +8,7 @@
 ROW_BLOCK = 128
 LANES = 128
 TILE = 384
-VMEM_LIMIT = 60 * 1024 * 1024
+VMEM_LIMIT = 48 * 1024 * 1024
 MESH = pl.DeviceIdType.MESH
 
 epsilon = 1e-06
@@ -41,10 +39,10 @@
 def main_kernel(
     pilots_hbm, estimate_hbm, visible_hbm, blocks_hbm, received_hbm, previous_hbm, onsager_hbm,
     labels_hbm, prior_hbm,
-    resid_hbm, scaled_hbm, nearby_hbm,
+    fresh_out, resid_out, owned_out,
     pilots, estimate, visible, blocks, received, previous, onsager, labels, prior,
-    resid_out, scaled, nearby, selector, window, swapped, half, arrived, owned,
-    load_sem, pilot_sem, store_sem, swap_sem, sum_send, sum_recv, post_send, post_recv,
+    scaled, nearby, selector, window, swapped, half, arrived, owned,
+    load_sem, pilot_sem, swap_sem, sum_send, sum_recv, post_send, post_recv,
 ):
     regions, clusters = lax.axis_size("region"), lax.axis_size("cluster")
     region, cluster = lax.axis_index("region"), lax.axis_index("cluster")
@@ -105,25 +103,27 @@
 
     loads[0].wait()
     row_id, lane_id = window_places(visible[...], users, rows)
+    for copy in loads[1:]:
+        copy.wait()
+    slot_block = lax.broadcasted_iota(jnp.int32, (1, slots), 1) // ROW_BLOCK
+    first_pass = []
     for point in range(points):
+        live = slot_block < blocks[0:1, point : point + 1]
+        widened = jnp.where(live, estimate[point].astype(jnp.float32), 0.0)
+        masked = widened.astype(jnp.bfloat16)
+        onward = received[point] + onsager[0:1, point : point + 1] * previous[point]
+        fetches[point].wait()
+        product = jnp.dot(masked, pilots[point], preferred_element_type=jnp.float32)
         for start in range(0, 2 * half_rows, TILE):
             selector[pl.ds(start, TILE), pl.ds(point * slots, slots)] = jnp.where(
                 one_hot(row_id[point : point + 1], TILE, start), 1.0, 0.0
             ).astype(jnp.bfloat16)
-    for copy in loads[1:]:
-        copy.wait()
-    slot_block = lax.broadcasted_iota(jnp.int32, (1, slots), 1) // ROW_BLOCK
-    for point in range(points):
-        live = slot_block < blocks[0:1, point : point + 1]
-        widened = jnp.where(live, estimate[point].astype(jnp.float32), 0.0)
-        masked = widened.astype(jnp.bfloat16)
-        fetches[point].wait()
-        product = jnp.dot(masked, pilots[point], preferred_element_type=jnp.float32)
-        resid = received[point] - product + onsager[0:1, point : point + 1] * previous[point]
+        resid = onward - product
         resid_out[point] = resid
         square = jnp.sum(jnp.sum(resid * resid, axis=0, keepdims=True), axis=1, keepdims=True)
         spread = square / (antennas * resid.shape[1]) + epsilon
-        narrow = resid.astype(jnp.bfloat16)
+        first_pass.append((live, widened, resid.astype(jnp.bfloat16), spread))
+    for point, (live, widened, narrow, spread) in enumerate(first_pass):
         stat = widened + lax.dot_general(
             narrow, pilots[point], (((1,), (1,)), ((), ())), preferred_element_type=jnp.float32
         )
@@ -161,12 +161,6 @@
 
     first = swap(side(window, 1 - core), swapped, 0)
     first.start()
-    stores = [
-        pltpu.make_async_copy(resid_out, resid_hbm, store_sem.at[0]),
-        pltpu.make_async_copy(scaled, scaled_hbm, store_sem.at[1]),
-    ]
-    for copy in stores:
-        copy.start()
     total = jnp.zeros(owned.shape, jnp.float32)
     for k in range(prior.shape[1]):
         total = total + jnp.where(labels[...] == k, prior[0:1, k : k + 1], 0.0)
@@ -201,6 +195,7 @@
 
     posterior = jax.nn.sigmoid(lax.fori_loop(1, peers, collect, total))
     owned[...] = posterior
+    owned_out[...] = posterior
 
     @pl.loop(1, peers)
     def _(j):
@@ -221,66 +216,40 @@
         recv_sem=swap_sem.at[3], device_id=partner, device_id_type=MESH,
     )
     waiting.wait_recv()
-    finish = pltpu.make_async_copy(nearby, nearby_hbm, store_sem.at[2])
-    finish.start()
-
-    @pl.loop(1, peers)
-    def _(j):
-        slot, back, device = peer(j)
-        sum_copy(slot, back, device).wait_send()
-        post_copy(slot, back, device).wait_send()
-
-    first.wait_send()
-    last.wait_send()
-    for copy in stores:
-        copy.wait()
-    finish.wait()
-
-
-def denoise_kernel(
-    users, visible_hbm, scaled_hbm, nearby_hbm, resid_hbm, fresh_hbm, resid_out, owned_out,
-    visible, scaled, nearby, fresh, sem, store_sem,
-):
-    clusters, cluster = lax.axis_size("cluster"), lax.axis_index("cluster")
-    rows = owned_out.shape[0]
-    points = visible.shape[0]
-    place = lax.rem(cluster, 2) * (3 * clusters // 2) + clusters // 2 + lax.div(cluster, 2)
-    own_rows = pl.ds(pl.multiple_of(place * rows, rows), rows)
-    copies = [
-        pltpu.make_async_copy(source, target, sem.at[i])
-        for i, (source, target) in enumerate(
-            [
-                (visible_hbm, visible), (nearby_hbm, nearby), (scaled_hbm, scaled),
-                (resid_hbm, resid_out), (nearby_hbm.at[own_rows, :], owned_out),
-            ]
-        )
-    ]
-    for copy in copies:
-        copy.start()
-    copies[0].wait()
-    row_id, lane_id = window_places(visible[...], users, rows)
-    copies[1].wait()
     table = jnp.concatenate(halves(nearby[...]), axis=1)
-    copies[2].wait()
-    stores = []
     for point in range(points):
         picked = None
-        for start in range(0, nearby.shape[0], TILE):
-            hot = jnp.where(one_hot(row_id[point : point + 1], TILE, start), 1.0, 0.0)
+        for start in range(0, 2 * half_rows, TILE):
             term = lax.dot_general(
-                table[start : start + TILE], hot.astype(jnp.bfloat16), (((0,), (0,)), ((), ())),
-                preferred_element_type=jnp.float32,
+                table[start : start + TILE],
+                selector[pl.ds(start, TILE), pl.ds(point * slots, slots)],
+                (((0,), (0,)), ((), ())), preferred_element_type=jnp.float32,
             )
             picked = term if picked is None else picked + term
         picked = picked[:LANES] + picked[LANES:]
         lanes = one_hot(lane_id[point : point + 1], LANES)
         rate = jnp.sum(jnp.where(lanes, picked, 0.0), axis=0, keepdims=True)
-        fresh[point] = (rate * scaled[point]).astype(jnp.bfloat16)
-        stores.append(
-            pltpu.make_async_copy(fresh.at[point], fresh_hbm.at[point], store_sem.at[point])
-        )
-        stores[-1].start()
-    for copy in copies[3:] + stores:
+        fresh_out[point] = (rate * scaled[point]).astype(jnp.bfloat16)
+
+    @pl.loop(1, peers)
+    def _(j):
+        slot, back, device = peer(j)
+        sum_copy(slot, back, device).wait_send()
+        post_copy(slot, back, device).wait_send()
+
+    first.wait_send()
+    last.wait_send()
+
+
+def store_kernel(fresh, resid, owned, fresh_hbm, resid_hbm, owned_hbm, sem):
+    copies = [
+        pltpu.make_async_copy(resid, resid_hbm, sem.at[0]),
+        pltpu.make_async_copy(fresh, fresh_hbm, sem.at[1]),
+        pltpu.make_async_copy(owned, owned_hbm, sem.at[2]),
+    ]
+    for copy in copies:
+        copy.start()
+    for copy in copies:
         copy.wait()
 
 
@@ -295,17 +264,19 @@
     peers = 3 * clusters // 2
     half_rows = peers * rows
     f32, i32, bf16 = jnp.float32, jnp.int32, jnp.bfloat16
-    place = pl.BlockSpec(memory_space=pl.ANY)
-    shape, vmem, dma = jax.ShapeDtypeStruct, pltpu.VMEM, pltpu.SemaphoreType.DMA
-    resid, scaled, nearby = pl.pallas_call(
+    kept = pl.BlockSpec(memory_space=pltpu.HBM)
+    near = pl.BlockSpec(memory_space=pltpu.VMEM)
+    vmem, dma = pltpu.VMEM, pltpu.SemaphoreType.DMA
+    results = [
+        ((points, antennas, slots), bf16),
+        ((points, antennas, length), f32),
+        ((rows, LANES), f32),
+    ]
+    made = pl.pallas_call(
         main_kernel,
-        in_specs=[place] * 9,
-        out_specs=[place] * 3,
-        out_shape=[
-            shape((points, antennas, length), f32),
-            shape((points, antennas, slots), f32),
-            shape((2 * half_rows, LANES), f32),
-        ],
+        in_specs=[kept] * 9,
+        out_specs=[near] * 3,
+        out_shape=[pltpu.VMEM(*result) for result in results],
         scratch_shapes=[
             vmem((points, slots, length), bf16),
             vmem((points, antennas, slots), bf16),
@@ -316,7 +287,6 @@
             vmem((1, points), f32),
             vmem((rows, LANES), i32),
             vmem((1, cluster_prior.shape[0]), f32),
-            vmem((points, antennas, length), f32),
             vmem((points, antennas, slots), f32),
             vmem((2 * half_rows, LANES), f32),
             vmem((2 * half_rows, points * slots), bf16),
@@ -325,34 +295,29 @@
             vmem((half_rows, LANES), f32),
             vmem((half_rows, LANES), f32),
             vmem((rows, LANES), f32),
-            dma((8,)), dma((points,)), dma((3,)), dma((4,)),
+            dma((8,)), dma((points,)), dma((4,)),
             dma((peers,)), dma((peers,)), dma((peers,)), dma((peers,)),
         ],
         compiler_params=pltpu.CompilerParams(
             collective_id=0, has_side_effects=True, vmem_limit_bytes=VMEM_LIMIT
         ),
     )(
-        pilots, estimate, visible, blocks.reshape(1, -1), received, previous,
-        onsager.reshape(1, -1), user_cluster.reshape(-1, LANES), cluster_prior.reshape(1, -1),
+        *[
+            pltpu.with_memory_space_constraint(operand, pltpu.HBM)
+            for operand in (
+                pilots, estimate, visible, blocks.reshape(1, -1), received, previous,
+                onsager.reshape(1, -1), user_cluster.reshape(-1, LANES),
+                cluster_prior.reshape(1, -1),
+            )
+        ]
     )
     new_estimate, resid, owned = pl.pallas_call(
-        functools.partial(denoise_kernel, users),
-        in_specs=[place] * 4,
-        out_specs=[place] * 3,
-        out_shape=[
-            shape((points, antennas, slots), bf16),
-            shape((points, antennas, length), f32),
-            shape((rows, LANES), f32),
-        ],
-        scratch_shapes=[
-            vmem((points, slots), i32),
-            vmem((points, antennas, slots), f32),
-            vmem((2 * half_rows, LANES), f32),
-            vmem((points, antennas, slots), bf16),
-            dma((5,)), dma((points,)),
-        ],
-        compiler_params=pltpu.CompilerParams(vmem_limit_bytes=VMEM_LIMIT),
-    )(visible, scaled, nearby, resid)
+        store_kernel,
+        in_specs=[near] * 3,
+        out_specs=[kept] * 3,
+        out_shape=[pltpu.HBM(*result) for result in results],
+        scratch_shapes=[dma((3,))],
+    )(*[pltpu.with_memory_space_constraint(result, pltpu.VMEM) for result in made])
     return (new_estimate, resid, owned.reshape(-1))
 
 

time: 31.5 us -> 28 us (0.89)
  Pallas kernels: 30.5 us -> 27.1 us
    pallas_call x2, Pallas kernels: 30.5 us -> 27.1 us  [the longest x1 26.4 us: local(): pl.pallas_call(main_kernel, in_specs=[kept] * 9, out_specs=[near] * 3, ou...]
where the time goes in v3:
time: 28 us; the launch traced here: 27.7 us
  Pallas kernels  27.1 us (97%)
  between operations  0.64 us (2%)
    pallas_call x1, Pallas kernels, local(): pl.pallas_call(main_kernel, in_specs=[kept] * 9, out_specs=[near] * 3, ou...  26.4 us
    pallas_call x1, Pallas kernels, local(): pl.pallas_call(store_kernel, in_specs=[near] * 3, out_specs=[kept] * 3, o...  0.7 us

profile of v3, /device:TPU:1, one launch (start us, length us, event | category | flops | bytes accessed | tf_op | source)
XLA Modules:
  0.0 27.7 jit_solution(16313019668237415140)
XLA Ops:
  0.6 26.4 %shard_map.112 = (bf16[4,8,1024]{2,1,0:T(8,128)(2,1)S(1)}, f32[4,8,1024]{2,1,0:T(8,128)S(1)}, f32[16,128]{1,0:T(8,128)S(1)}) custom-call(bf16[4,1024,1024]{2,1,0:T(8,128)(2,1)} %pilots_hbm.1, bf16[4,8,1024]{2,1,0:T(8,128)(2,1)} %estimate_hbm.1, s32[4,1024]{1,0:T(4,128)} %visible_hbm.1, s32[1,4]{1,0:T(1,128)} %bitcast.6, f32[4,8,1024]{2,1,0:T(8,128)} %received_hbm.1, ...), custom_call_target="tpu_custom_call" | custom-call | tf_op jit(solution)/shard_map/pallas_call | solution.py:275
  27.0 0.7 %shard_map.113 = (bf16[4,8,1024]{2,1,0:T(8,128)(2,1)}, f32[4,8,1024]{2,1,0:T(8,128)}, f32[16,128]{1,0:T(8,128)}) custom-call(bf16[4,8,1024]{2,1,0:T(8,128)(2,1)S(1)} %get-tuple-element.9.fresh, f32[4,8,1024]{2,1,0:T(8,128)S(1)} %get-tuple-element.10.resid, f32[16,128]{1,0:T(8,128)S(1)} %get-tuple-element.11.owned), custom_call_target="tpu_custom_call" | custom-call | tf_op jit(solution)/shard_map/pallas_call | solution.py:314

commit v4 on v3

--- a/solution.py
+++ b/solution.py
@@ -215,8 +215,14 @@
         src_ref=side(nearby, core), dst_ref=side(nearby, 1 - core), send_sem=swap_sem.at[2],
         recv_sem=swap_sem.at[3], device_id=partner, device_id_type=MESH,
     )
+    @pl.loop(1, peers)
+    def _(j):
+        slot, back, device = peer(j)
+        sum_copy(slot, back, device).wait_send()
+        post_copy(slot, back, device).wait_send()
+
     waiting.wait_recv()
-    table = jnp.concatenate(halves(nearby[...]), axis=1)
+    table = nearby[...].astype(jnp.bfloat16)
     for point in range(points):
         picked = None
         for start in range(0, 2 * half_rows, TILE):
@@ -226,16 +232,9 @@
                 (((0,), (0,)), ((), ())), preferred_element_type=jnp.float32,
             )
             picked = term if picked is None else picked + term
-        picked = picked[:LANES] + picked[LANES:]
         lanes = one_hot(lane_id[point : point + 1], LANES)
         rate = jnp.sum(jnp.where(lanes, picked, 0.0), axis=0, keepdims=True)
         fresh_out[point] = (rate * scaled[point]).astype(jnp.bfloat16)
-
-    @pl.loop(1, peers)
-    def _(j):
-        slot, back, device = peer(j)
-        sum_copy(slot, back, device).wait_send()
-        post_copy(slot, back, device).wait_send()
 
     first.wait_send()
     last.wait_send()

time: 28 us -> 27.3 us (0.975)
  Pallas kernels: 27.1 us -> 26.4 us
    pallas_call x1, Pallas kernels: 26.4 us -> 25.7 us  [local(): pl.pallas_call(main_kernel, in_specs=[kept] * 9, out_specs=[near] * 3, ou...]
where the time goes in v4:
time: 27.3 us; the launch traced here: 27 us
  Pallas kernels  26.4 us (97%)
  between operations  0.64 us (2%)
    pallas_call x1, Pallas kernels, local(): pl.pallas_call(main_kernel, in_specs=[kept] * 9, out_specs=[near] * 3, ou...  25.7 us
    pallas_call x1, Pallas kernels, local(): pl.pallas_call(store_kernel, in_specs=[near] * 3, out_specs=[kept] * 3, o...  0.7 us

profile of v4, /device:TPU:1, one launch (start us, length us, event | category | flops | bytes accessed | tf_op | source)
XLA Modules:
  0.0 27.0 jit_solution(6599690102437602083)
XLA Ops:
  0.6 25.7 %shard_map.112 = (bf16[4,8,1024]{2,1,0:T(8,128)(2,1)S(1)}, f32[4,8,1024]{2,1,0:T(8,128)S(1)}, f32[16,128]{1,0:T(8,128)S(1)}) custom-call(bf16[4,1024,1024]{2,1,0:T(8,128)(2,1)} %pilots_hbm.1, bf16[4,8,1024]{2,1,0:T(8,128)(2,1)} %estimate_hbm.1, s32[4,1024]{1,0:T(4,128)} %visible_hbm.1, s32[1,4]{1,0:T(1,128)} %bitcast.6, f32[4,8,1024]{2,1,0:T(8,128)} %received_hbm.1, ...), custom_call_target="tpu_custom_call" | custom-call | tf_op jit(solution)/shard_map/pallas_call | solution.py:274
  26.3 0.7 %shard_map.113 = (bf16[4,8,1024]{2,1,0:T(8,128)(2,1)}, f32[4,8,1024]{2,1,0:T(8,128)}, f32[16,128]{1,0:T(8,128)}) custom-call(bf16[4,8,1024]{2,1,0:T(8,128)(2,1)S(1)} %get-tuple-element.9.fresh, f32[4,8,1024]{2,1,0:T(8,128)S(1)} %get-tuple-element.10.resid, f32[16,128]{1,0:T(8,128)S(1)} %get-tuple-element.11.owned), custom_call_target="tpu_custom_call" | custom-call | tf_op jit(solution)/shard_map/pallas_call | solution.py:313
